TPU v7x, 128 devices: a whole 4x4x4 slice. The times are simulated.
128 devices in a mesh: ctx: 16 (over x, y_lo, core), ch: 8 (over y_hi, z).
Axes of the slice: x: 4, y: 4 (y_hi: 2, y_lo: 2; y = y_hi * 2 + y_lo), z: 4, core: 2. Of those that a mesh axis runs over, the one named last changes fastest.
Arguments:
- query_in: bfloat16 [3072, 8192], P('ctx', 'ch'), may hold values from -6 to 6
- key_in: bfloat16 [3072, 8192], P('ctx', 'ch'), may hold values from -6 to 6
- value_in: bfloat16 [3072, 8192], P('ctx', 'ch'), may hold values from -6 to 6
- filters: bfloat16 [512, 3072], P('ch'), may hold values from -0.8 to 0.8
- skip_gain: float32 [8192], P('ch'), may hold values from -3 to 3
- out_weight: bfloat16 [8192, 8192], P(None, 'ch'), may hold values from -0.0625 to 0.0625
Outputs:
- output: bfloat16 [3072, 8192], P('ctx', 'ch')
All inputs are finite; a program needn't handle non-finite values.
Results may differ from a plain program's by a relative error of at most 0.0057.
Values may be sent and summed in bfloat16 or wider, within the bound.
No kernel may reach another device: no remote copies, remote signals or barrier semaphores. Data moves between devices by JAX's collectives and lax.ppermute only.
A program may use at most 128 MiB of HBM per device.

v0:
```python
import jax
import jax.numpy as jnp
from jax import lax
from jax.sharding import PartitionSpec as P


def toeplitz(padded, offset, out_rows, src_rows):
    groups = padded.shape[0]
    seq_len = padded.shape[1] // 2
    width = out_rows + src_rows - 1
    segment = lax.dynamic_slice_in_dim(padded, offset - src_rows + 1 + seq_len, width, 1)
    flipped = jnp.concatenate([segment[:, ::-1], jnp.zeros((groups, 1), segment.dtype)], axis=1)
    period = width + 1
    repeated = jnp.broadcast_to(flipped[:, None, :], (groups, out_rows, period)).reshape(
        groups, out_rows * period
    )
    sheared = repeated[:, out_rows - 1 : out_rows - 1 + out_rows * width].reshape(
        groups, out_rows, width
    )
    return sheared[:, :, :src_rows]


def conv_term(padded, offset, out_rows, source):
    tiles = toeplitz(padded, offset, out_rows, source.shape[0])
    grouped = source.reshape(source.shape[0], padded.shape[0], -1)
    result = jnp.einsum("grs,sgc->rgc", tiles, grouped, preferred_element_type=jnp.float32)
    return result.reshape(out_rows, -1)


def causal_add(summed, padded, out_start, out_rows, source, src_start):

    def include(current):
        return current + conv_term(padded, out_start - src_start, out_rows, source)

    def leave(current):
        return current

    return lax.cond(src_start < out_start + out_rows, include, leave, summed)


def apply_gate(query_part, conv, gain, mixed_part):
    total = conv + gain[None, :] * mixed_part.astype(jnp.float32)
    return (query_part.astype(jnp.float32) * total).astype(jnp.bfloat16)


def project(gated, out_weight):
    total = jnp.dot(
        lax.all_gather(gated, "ch", axis=1, tiled=True),
        out_weight,
        preferred_element_type=jnp.float32,
    )
    return total.astype(jnp.bfloat16)


def shards(query_in, key_in, value_in, filters, skip_gain, out_weight):
    block_rows = query_in.shape[0]
    channels = query_in.shape[1]
    cycle_pos = lax.axis_index("ctx")
    mixed = (key_in.astype(jnp.float32) * value_in.astype(jnp.float32)).astype(jnp.bfloat16)
    padded = jnp.concatenate([jnp.zeros_like(filters), filters], axis=1)
    out_start = cycle_pos * block_rows
    empty = jnp.zeros((block_rows, channels), jnp.float32)
    portion = lax.all_gather(mixed, "ctx", axis=0, tiled=True)
    height = portion.shape[0]
    pieces = portion.reshape(height // block_rows, block_rows, channels)

    def advance(running, element):
        position, piece = element
        return (
            causal_add(running, padded, out_start, block_rows, piece, position * block_rows),
            None,
        )

    running, _ = lax.scan(
        advance, empty, (jnp.arange(height // block_rows, dtype=jnp.int32), pieces)
    )
    return project(apply_gate(query_in, running, skip_gain, mixed), out_weight)


def solution(mesh):
    placed = (P("ctx", "ch"), P("ctx", "ch"), P("ctx", "ch"), P("ch", None), P("ch"), P(None, "ch"))
    return jax.shard_map(
        shards, mesh=mesh, in_specs=placed, out_specs=P("ctx", "ch"), check_vma=False
    )
```

profile of v0, /device:TPU:0, one launch (start us, length us, event | category | flops | bytes accessed | tf_op | source)
XLA Modules:
  0.0 1123.3 jit_solution(5549705480522828979)
XLA Ops:
  6.5 0.0 all-gather.3.cloned.1.call-start
  6.5 2.0 multiply_convert_fusion.1
  8.5 0.0 all-gather.3.cloned.1.call-update
  8.6 0.0 all-gather.5.cloned.1.call-start
  8.6 1.1 concatenate.6
  9.7 44.2 %all-gather.3.cloned.1.call-done = bf16[3072,1024]{1,0:T(8,128)(2,1)} async-done(((bf16[192,1024]{1,0:T(8,128)(2,1)}), bf16[3072,1024]{1,0:T(8,128)(2,1)}) %all-gather.3.cloned.1.call-update) | async-done | bytes 6291472 | tf_op jit(solution)/shard_map/all_gather | solution.py:63
  53.9 11.0 copy.11
  64.9 0.1 broadcast_in_dim.5
  65.0 0.0 copy-start
  65.0 0.0 copy-start.1
  65.0 0.0 copy-start.2
  65.0 81.9 %while.14 = (s32[]{:T(128)}, f32[192,1024]{0,1:T(8,128)S(1)}, s32[16]{0:T(128)S(1)}, s32[]{:T(128)}, s32[]{:T(128)}, /*index=5*/bf16[64,6144]{1,0:T(8,128)(2,1)S...) while((s32[]{:T(128)}, f32[192,1024]{0,1:T(8,128)S(1)}, s32[16]{0:T(128)S(1)}, s32[]{:T(128)}, ...), condition=%wide.region_3.4_spmd, body=%wide.region_0.3_spmd.sunk | while | flops 75694096 | bytes 77020792 | solution.py:74
  65.0 0.7 dynamic_slice.19
  66.4 59.7 %conditional.2 = (f32[192,1024]{0,1:T(8,128)S(1)}) conditional(s32[]{:T(128)} %convert_element_type.40, f32[192,1024]{0,1:T(8,128)S(1)} %get-tuple-element.186, (s32[]{:T(128)}, s32[]{:T(128)}, bf16[64,6144]{1,0:T(8,128)(2,1)S(1)}, bf16[16,192,1024]{1,2,0:T(8,128)(2,1)}, s32[]{:T(128)}, /*index=5*/f32[192,1024]{0,1:T(8,128)S(1)}) %tuple.35), branch_computations={%region_1.1_spmd, %region_2.2_spmd} | conditional | flops 75694088 | bytes 77020616 | solution.py:38
  66.4 0.1 constant_dynamic-slice_fusion.1
  66.5 0.3 reverse
  66.7 0.1 slice.12
  66.9 4.5 broadcast_in_dim.1
  71.3 13.3 %copy.13 = bf16[8,8,192,384]{3,1,2,0:T(8,128)(2,1)} copy(bf16[8,8,192,384]{3,2,1,0:T(8,128)(2,1)} %bitcast.15) | data formatting | bytes 18874368 | tf_op jit(solution)/shard_map/while/body/eval_jaxpr/cond
  84.7 9.8 slice.8
  94.5 25.7 %reshape.21 = bf16[64,192,383]{2,1,0:T(8,128)(2,1)} reshape(bf16[64,73536]{1,0:T(8,128)(2,1)} %slice.8) | data formatting | bytes 18825216 | tf_op jit(solution)/shard_map/while/body/eval_jaxpr/cond/branch_1_fun/reshape | solution.py:17
  120.2 1.1 constant_dynamic-slice_fusion
  121.3 4.5 fusion
  125.8 0.2 bitcast_add_fusion
  126.1 0.7 dynamic_slice.19
  127.4 0.7 dynamic_slice.19
  128.8 0.7 dynamic_slice.19
  130.2 0.7 dynamic_slice.19
  131.6 0.7 dynamic_slice.19
  132.9 0.7 dynamic_slice.19
  134.3 0.7 dynamic_slice.19
  135.7 0.7 dynamic_slice.19
  137.1 0.7 dynamic_slice.19
  138.4 0.7 dynamic_slice.19
  139.8 0.7 dynamic_slice.19
  141.2 0.7 dynamic_slice.19
  142.6 0.7 dynamic_slice.19
  143.9 0.7 dynamic_slice.19
  145.3 0.7 dynamic_slice.19
  146.9 0.3 copy.12
  147.2 0.0 copy-done
  147.2 0.0 copy-done.1
  147.2 0.0 copy-done.2
  147.2 0.9 multiply_convert_fusion
  148.1 0.0 all-gather.5.cloned.1.call-update
  148.2 957.4 %all-gather.5.cloned.1.call-done = bf16[192,8192]{1,0:T(8,128)(2,1)} async-done(((bf16[192,1024]{1,0:T(8,128)(2,1)}), bf16[192,8192]{1,0:T(8,128)(2,1)}) %all-gather.5.cloned.1.call-update) | async-done | bytes 3145744 | tf_op jit(solution)/shard_map/all_gather | solution.py:48
  1105.6 10.9 convolution_convert_fusion
  (17 shorter events, 0.2 us)
Async XLA Ops:
  6.5 47.3 %all-gather.3.cloned.1.call-start = ((), (), s32[]{:S(2)}) async-start(), calls=%async_computation | async-start | bytes 6684672 | tf_op jit(solution)/shard_map/all_gather | solution.py:63
  8.6 1097.0 %all-gather.5.cloned.1.call-start = ((), (), s32[]{:S(2)}) async-start(), calls=%async_computation.1 | async-start | bytes 3538944 | tf_op jit(solution)/shard_map/all_gather | solution.py:48
  65.0 82.2 %copy-start = (bf16[192,1024]{1,0:T(8,128)(2,1)S(1)}, bf16[192,1024]{1,0:T(8,128)(2,1)}, u32[]{:S(2)}) copy-start(bf16[192,1024]{1,0:T(8,128)(2,1)} %multiply_convert_fusion.1) | copy-start | bytes 1179652
  65.0 82.2 %copy-start.1 = (bf16[192,1024]{1,0:T(8,128)(2,1)S(1)}, bf16[192,1024]{1,0:T(8,128)(2,1)}, u32[]{:S(2)}) copy-start(bf16[192,1024]{1,0:T(8,128)(2,1)} %param.10) | copy-start | bytes 1179652
  65.0 82.2 %copy-start.2 = (f32[1024]{0:T(1024)S(1)}, f32[1024]{0:T(1024)}, u32[]{:S(2)}) copy-start(f32[1024]{0:T(1024)} %param.14) | copy-start | bytes 12292
Sparse Core Ops, SparseCore 0:
  9.0 44.7 all-gather.2
  148.3 957.2 all-gather.4
where the time goes:
time: 1130 us; the launch traced here: 1120 us
  waiting for transfers between devices  1000 us (88%)
  local copies, waits for them, and re-layouts  77.8 us (7%)
  matrix products  15.4 us (1%)
  between operations  13.5 us (1%)
  loops' own time  11.8 us (1%)
    all_gather x1, waiting for transfers between devices, project(): lax.all_gather(gated, 'ch', axis=1, tiled=True)  957 us
    all_gather x1, waiting for transfers between devices, shards(): portion = lax.all_gather(mixed, 'ctx', axis=0, tiled=True)  44.2 us
    reshape x1, local copies, waits for them, and re-layouts, toeplitz(): repeated[:, out_rows - 1:out_rows - 1 + out_rows * width]  25.7 us
  transfers between devices with their start and end apart: 2, of which 2 were waited for; matrix products, arithmetic and copies ran while one was open for 0% of the time, Pallas kernels for 0%

commit v1 on v0

v1 whole, which is shorter than its diff:
```python
import functools

import jax
import jax.numpy as jnp
from jax import lax
from jax.experimental import pallas as pl
from jax.experimental.pallas import tpu as pltpu
from jax.sharding import Mesh, PartitionSpec as P


CTX = ("x", "ylo", "core")
CH = ("yhi", "z")
FRONT = 256
BACK = 128
TALL = 16
LANES = 128
NT = (((1,), (1,)), ((), ()))
MIB = 1 << 20
WHOLE = pl.BlockSpec(memory_space=pltpu.VMEM)
FAR = pl.BlockSpec(memory_space=pltpu.HBM)
DMA = pltpu.SemaphoreType.DMA


def near(array):
    return pltpu.with_memory_space_constraint(array, pltpu.VMEM)


def far(array):
    return pltpu.with_memory_space_constraint(array, pltpu.HBM)


def params(mib):
    return pltpu.CompilerParams(vmem_limit_bytes=mib * MIB)


def places(shape, dimension):
    return lax.broadcasted_iota(jnp.int32, shape, dimension)


def identity(size):
    shape = (size, size)
    return (places(shape, 0) == places(shape, 1)).astype(jnp.bfloat16)


def ctx_index():
    return (lax.axis_index("x") * 2 + lax.axis_index("ylo")) * 2 + lax.axis_index("core")


def mix_kernel(key_ref, value_ref, out_ref, keys, values, sems):
    rows, width = keys.shape
    parts = out_ref.shape[0]
    pieces = 4
    step = width // pieces
    copies = []
    for n in range(pieces):
        at = pl.ds(n * step, step)
        pair = (
            pltpu.make_async_copy(key_ref.at[:, at], keys.at[:, at], sems.at[0, n]),
            pltpu.make_async_copy(value_ref.at[:, at], values.at[:, at], sems.at[1, n]),
        )
        for copy in pair:
            copy.start()
        copies.append(pair)
    unit = identity(step)
    own = width // parts
    for n, pair in enumerate(copies):
        for copy in pair:
            copy.wait()
        at = slice(n * step, (n + 1) * step)
        product = keys[:, at].astype(jnp.float32) * values[:, at].astype(jnp.float32)
        turned = lax.dot_general(
            unit, product.astype(jnp.bfloat16), NT, preferred_element_type=jnp.float32
        )
        turned = turned.astype(jnp.bfloat16).reshape(step // own, own, rows)
        here = slice(n * step // own, (n + 1) * step // own)
        out_ref[here, :own, :] = turned[:, :, :LANES]
        half = own // 2
        tail = turned[:, :, LANES:]
        out_ref[here, own:, :] = jnp.concatenate([tail[:, :half], tail[:, half:]], axis=2)


def mix(key_in, value_in, parts):
    rows, channels = key_in.shape
    return pl.pallas_call(
        mix_kernel,
        out_shape=pltpu.VMEM((parts, channels * rows // parts // LANES, LANES), jnp.bfloat16),
        in_specs=[FAR, FAR],
        out_specs=WHOLE,
        scratch_shapes=[
            pltpu.VMEM((rows, channels), jnp.bfloat16),
            pltpu.VMEM((rows, channels), jnp.bfloat16),
            DMA((2, 4)),
        ],
        compiler_params=params(6),
        name="mix",
    )(far(key_in), far(value_in))


def taps_kernel(filters_ref, out_ref, held, sem):
    fetch = pltpu.make_async_copy(filters_ref, held, sem)
    fetch.start()
    fetch.wait()
    groups = held.shape[0]
    own = out_ref.shape[0]
    base = ctx_index() * own

    @pl.loop(0, own)
    def _(g):
        pick = places((TALL, groups), 1) == base + g
        taps = jnp.dot(
            pick.astype(jnp.bfloat16), held[...], preferred_element_type=jnp.float32
        )
        front = jnp.zeros((TALL, FRONT), jnp.float32)
        line = jnp.concatenate([front, taps, jnp.zeros((TALL, BACK), jnp.float32)], axis=1)
        row = places(line.shape, 0)
        for bit in (1, 2, 4, 8):
            line = jnp.where((row & bit) != 0, pltpu.roll(line, bit, 1), line)
        for shift in range(8):
            moved = line if shift == 0 else pltpu.roll(line, TALL * shift, 1)
            out_ref[g, shift] = moved.astype(jnp.bfloat16)


def spread_taps(filters, parts):
    groups, seq = filters.shape
    own = groups // parts
    width = FRONT + seq + BACK
    return pl.pallas_call(
        taps_kernel,
        out_shape=pltpu.VMEM((own, 8, TALL, width), jnp.bfloat16),
        in_specs=[FAR],
        out_specs=WHOLE,
        scratch_shapes=[pltpu.VMEM(filters.shape, filters.dtype), DMA],
        compiler_params=params(8),
        cost_estimate=pl.CostEstimate(
            flops=2 * TALL * groups * seq * own, bytes_accessed=8 * MIB, transcendentals=0
        ),
        name="taps",
    )(far(filters))


def conv_kernel(x_ref, taps_ref, gain_ref, query_ref, out_ref, held_ref, acc_ref, gains, sems):
    first = pltpu.make_async_copy(gain_ref, gains, sems.at[0])
    fetch = pltpu.make_async_copy(query_ref, held_ref, sems.at[1])
    first.start()
    fetch.start()
    blocks = x_ref.shape[0]
    own, _, tall, _ = taps_ref.shape
    per_group = acc_ref.shape[0] // blocks
    channels = own * per_group
    rows = acc_ref.shape[1]
    base = ctx_index() * channels
    rest = rows - LANES

    @pl.loop(0, own // 2)
    def _(low):
        tails = []
        packed = x_ref[:, pl.ds(pl.multiple_of(channels + low * per_group, per_group), per_group), :]
        for high in range(2):
            g = high * 2 + low
            at = pl.multiple_of(g * per_group, per_group)
            piece = jnp.concatenate(
                [
                    x_ref[:, pl.ds(at, per_group), :],
                    packed[:, :, high * rest : (high + 1) * rest],
                ],
                axis=2,
            )
            acc_ref[...] = jnp.zeros_like(acc_ref)
            source = piece.reshape(blocks * per_group, rows)
            for lag in range(blocks):
                parts = []
                for k in range(rows // tall):
                    offset = FRONT + rows * lag - tall * k
                    shift = (-offset // tall) % 8
                    start = offset + tall * shift
                    parts.append(taps_ref[g, shift, :, start : start + rows])
                tile = jnp.concatenate(parts, axis=0)
                height = (blocks - lag) * per_group
                acc_ref[lag * per_group :, :] += jnp.dot(
                    source[:height], tile, preferred_element_type=jnp.float32
                )
            if high == 0:
                pl.when(low == 0)(first.wait)
            shape = (per_group, gains.shape[1])
            chosen = places(shape, 1) == base + at + places(shape, 0)
            gain = jnp.sum(jnp.where(chosen, gains[...], 0.0), axis=1, keepdims=True)
            total = acc_ref[...].reshape(blocks, per_group, rows)
            total = (total + piece.astype(jnp.float32) * gain[None]).astype(jnp.bfloat16)
            out_ref[:, pl.ds(at, per_group), :] = total[:, :, :LANES]
            tails.append(total[:, :, LANES:])
        here = pl.ds(pl.multiple_of(channels + low * per_group, per_group), per_group)
        out_ref[:, here, :] = jnp.concatenate(tails, axis=2)

    fetch.wait()


def convolve(x, taps, gain, query_in):
    blocks = x.shape[0]
    rows, channels = query_in.shape
    per_group = channels // blocks // taps.shape[0]
    return pl.pallas_call(
        conv_kernel,
        out_shape=(
            pltpu.VMEM(x.shape, jnp.bfloat16),
            pltpu.VMEM(query_in.shape, query_in.dtype),
        ),
        in_specs=[WHOLE, WHOLE, FAR, FAR],
        out_specs=(WHOLE, WHOLE),
        scratch_shapes=[
            pltpu.VMEM((blocks * per_group, rows), jnp.float32),
            pltpu.VMEM(gain.shape, gain.dtype),
            DMA((2,)),
        ],
        compiler_params=params(10),
        name="conv",
    )(near(x), near(taps), far(gain), far(query_in))


def gate_kernel(packed_ref, query_ref, out_ref):
    parts, _, _ = packed_ref.shape
    rows, width = query_ref.shape
    own = width // parts
    head = packed_ref[:, :own, :].reshape(width, LANES)
    tail = packed_ref[:, own:, :]
    tail = jnp.concatenate([tail, tail], axis=1).reshape(width, LANES)
    rest = rows - LANES
    upper = places(tail.shape, 0) // (own // 2) % 2
    tail = jnp.where(upper == places(tail.shape, 1) // rest, tail.astype(jnp.float32), 0.0)
    shape = (rest, LANES)
    fold = (places(shape, 1) % rest == places(shape, 0)).astype(jnp.bfloat16)
    for unit, turned, at in (
        (identity(LANES), head, slice(0, LANES)),
        (fold, tail.astype(jnp.bfloat16), slice(LANES, rows)),
    ):
        total = lax.dot_general(unit, turned, NT, preferred_element_type=jnp.float32)
        out_ref[at, :] = (query_ref[at, :].astype(jnp.float32) * total).astype(jnp.bfloat16)


def gate(packed, query_in):
    return pl.pallas_call(
        gate_kernel,
        out_shape=pltpu.VMEM(query_in.shape, jnp.bfloat16),
        in_specs=[WHOLE, WHOLE],
        out_specs=WHOLE,
        compiler_params=params(6),
        name="gate",
    )(near(packed), near(query_in))


def ring(size, step):
    return [(i, (i + step) % size) for i in range(size)]


def project_kernel(first, count, carried, *refs):
    refs = list(refs)
    blocks = [refs.pop(0) for _ in range(count)]
    slots = refs.pop(0)
    running = refs.pop(0) if carried else None
    (out_ref,) = refs
    width = out_ref.shape[1]
    tile = 256
    for m in range(0, width, tile):
        span = slice(m, m + tile)
        total = running[:, span] if carried else None
        for n, block in enumerate(blocks):
            part = jnp.dot(
                block[...], slots[first + n, :, span], preferred_element_type=jnp.float32
            )
            total = part if total is None else total + part
        out_ref[:, span] = total.astype(out_ref.dtype)


def project(first, blocks, slots, running, last):
    rows, depth = blocks[0].shape
    width = slots.shape[2]
    arrays = [near(block) for block in blocks] + [near(slots)]
    if running is not None:
        arrays.append(near(running))
    shape = (rows, width)
    return pl.pallas_call(
        functools.partial(project_kernel, first, len(blocks), running is not None),
        out_shape=(
            jax.ShapeDtypeStruct(shape, jnp.bfloat16) if last else pltpu.VMEM(shape, jnp.float32)
        ),
        in_specs=[WHOLE] * len(arrays),
        out_specs=WHOLE,
        compiler_params=params(4),
        cost_estimate=pl.CostEstimate(
            flops=2 * rows * depth * width * len(blocks),
            bytes_accessed=2 * depth * width * len(blocks),
            transcendentals=0,
        ),
        name="project",
    )(*arrays)


def fetch_kernel(weight_ref, slots_ref, sems):
    depth = slots_ref.shape[1]
    yhi, z = lax.axis_index("yhi"), lax.axis_index("z")
    pieces = sems.shape[1]
    step = depth // pieces
    copies = []
    for n, (side, back) in enumerate(OWNERS):
        owner = (yhi + side) % 2 * 4 + (z + 4 - back) % 4
        for m in range(pieces):
            at = pl.ds(pl.multiple_of(owner * depth + m * step, step), step)
            to = pl.ds(m * step, step)
            copies.append(
                pltpu.make_async_copy(weight_ref.at[at, :], slots_ref.at[n, to, :], sems.at[n, m])
            )
            copies[-1].start()
    for copy in copies:
        copy.wait()


def fetch(weight):
    count = len(OWNERS)
    shape = (count, weight.shape[0] // count, weight.shape[1])
    return pl.pallas_call(
        fetch_kernel,
        out_shape=pltpu.VMEM(shape, weight.dtype),
        in_specs=[FAR],
        out_specs=WHOLE,
        scratch_shapes=[DMA((count, 2))],
        compiler_params=params(2),
        cost_estimate=pl.CostEstimate(flops=0, bytes_accessed=2 * weight.size, transcendentals=0),
        name="fetch",
    )(far(weight))


def gather_project(gated, slots):
    def along(block, step):
        return lax.ppermute(block, "z", ring(4, step))

    def across(block):
        return lax.ppermute(block, "yhi", ring(2, 1))

    own = {2: along(gated, 2)}
    beyond = across(gated)
    own[1] = along(gated, 1)
    own[3] = along(gated, 3)
    other = {2: across(own[2])}
    other[1] = along(beyond, 1)
    other[3] = along(beyond, 3)
    total = project(0, [gated], slots, None, False)
    total = project(1, [own[2], beyond], slots, total, False)
    total = project(3, [own[1], own[3]], slots, total, False)
    total = project(5, [other[2]], slots, total, False)
    return project(6, [other[1], other[3]], slots, total, True)


def shards(query_in, key_in, value_in, filters, skip_gain, out_weight):
    parts = 16
    sent = mix(key_in, value_in, parts)
    whole = lax.all_to_all(sent, CTX, 0, 0, tiled=True)
    taps = spread_taps(filters, parts)
    slots = fetch(out_weight)
    total, query = convolve(whole, taps, skip_gain.reshape(1, -1), query_in)
    packed = lax.all_to_all(total, CTX, 0, 0, tiled=True)
    gated = gate(packed, query)
    return gather_project(gated, slots)


def solution(mesh):
    fine = Mesh(mesh.devices.reshape(4, 2, 2, 2, 4), CTX + CH)
    placed = (P(CTX, CH), P(CTX, CH), P(CTX, CH), P(CH, None), P(CH), P(None, CH))
    return jax.shard_map(
        shards, mesh=fine, in_specs=placed, out_specs=P(CTX, CH), check_vma=False
    )


OWNERS = ((0, 0), (0, 2), (1, 0), (0, 1), (0, 3), (1, 2), (1, 1), (1, 3))
```

time: 1130 us -> 66.3 us (0.06)
  waiting for transfers between devices: 1000 us -> 9.95 us
  local copies, waits for them, and re-layouts: 77.8 us -> 0 us
  starting transfers between devices: 0.04 us -> 22.2 us
  Pallas kernels: 0 us -> 21.9 us
  matrix products: 15.4 us -> 0 us
  between operations: 13.5 us -> 0.11 us
  loops' own time: 11.8 us -> 0 us
  blocking collectives: 0 us -> 11.7 us
    all_gather x2 -> x0, waiting for transfers between devices: 1000 us -> none  [the longest x1 957 us: project(): lax.all_gather(gated, 'ch', axis=1, tiled=True)]
    reshape x1 -> x0, local copies, waits for them, and re-layouts: 25.7 us -> none  [toeplitz(): repeated[:, out_rows - 1:out_rows - 1 + out_rows * width]]
    pallas_call x0 -> x10, Pallas kernels: none -> 21.9 us  [the longest x1 5.93 us: fetch(): pl.pallas_call(fetch_kernel, out_shape=pltpu.VMEM(shape, weight.dtype), i...]
    ppermute x0 -> x7, starting transfers between devices: none -> 16.7 us  [the longest x5 10.9 us: along(): return lax.ppermute(block, 'z', ring(4, step))]
    dot_general x2 -> x0, matrix products: 15.4 us -> none  [the longest x1 10.9 us: project(): jnp.dot(lax.all_gather(gated, 'ch', axis=1, tiled=True), out_weight, pref...]
    cond x3 -> x0, local copies, waits for them, and re-layouts: 13.7 us -> none
    another operation x17 -> x0, loops' own time: 11.8 us -> none  [the longest x1 11.6 us: shards(): lax.scan(advance, empty, (jnp.arange(height // block_rows, dtype=jnp.int3...]
    all_to_all x0 -> x1, blocking collectives: none -> 11.7 us  [shards(): packed = lax.all_to_all(total, CTX, 0, 0, tiled=True)]
  transfers between devices with their start and end apart: 2 -> 8, of which waited for: 2 -> 4; matrix products, arithmetic and copies ran while one was open for 0% -> 0% of each run, Pallas kernels for 0% -> 20%
where the time goes in v1:
time: 66.3 us; the launch traced here: 65.9 us
  starting transfers between devices  22.2 us (33%)
  Pallas kernels  21.9 us (33%)
  blocking collectives  11.7 us (18%)
  waiting for transfers between devices  9.95 us (15%)
    all_to_all x1, blocking collectives, shards(): packed = lax.all_to_all(total, CTX, 0, 0, tiled=True)  11.7 us
    ppermute x5, starting transfers between devices, along(): return lax.ppermute(block, 'z', ring(4, step))  10.9 us
    pallas_call x1, Pallas kernels, fetch(): pl.pallas_call(fetch_kernel, out_shape=pltpu.VMEM(shape, weight.dtype), i...  5.93 us
    ppermute x2, starting transfers between devices, across(): return lax.ppermute(block, 'yhi', ring(2, 1))  5.74 us
    all_to_all x1, starting transfers between devices, shards(): whole = lax.all_to_all(sent, CTX, 0, 0, tiled=True)  5.59 us
    ppermute x5, waiting for transfers between devices, along(): return lax.ppermute(block, 'z', ring(4, step))  4.98 us
    all_to_all x1, waiting for transfers between devices, shards(): whole = lax.all_to_all(sent, CTX, 0, 0, tiled=True)  4.96 us
    pallas_call x5, Pallas kernels, project(): pl.pallas_call(functools.partial(project_kernel, first, len(blocks), runn...  4.9 us
  transfers between devices with their start and end apart: 8, of which 4 were waited for; matrix products, arithmetic and copies ran while one was open for 0% of the time, Pallas kernels for 20%

profile of v1, /device:TPU:0, one launch (start us, length us, event | category | flops | bytes accessed | tf_op | source)
XLA Modules:
  0.0 65.9 jit_solution(15815084292771882311)
XLA Ops:
  0.0 3.0 %mix.1 = bf16[16,96,128]{2,1,0:T(8,128)(2,1)} custom-call(bf16[192,1024]{1,0:T(8,128)(2,1)} %key_ref.1, bf16[192,1024]{1,0:T(8,128)(2,1)} %value_ref.1), custom_call_target="tpu_custom_call" | custom-call | tf_op jit(solution)/shard_map/mix/pallas_call | solution.py:84
  3.0 5.6 %all-to-all-start = ((bf16[16,96,128]{2,1,0:T(8,128)(2,1)}), bf16[16,96,128]{2,1,0:T(8,128)(2,1)}, u32[]{:S(2)}, u32[]{:S(2)}) async-start(bf16[16,96,128]{2,1,0:T(8,128)(2,1)} %mix.1), calls=%async_computation | async-start | bytes 786432 | tf_op jit(solution)/shard_map/all_to_all | solution.py:355
  8.6 4.2 %taps.1.taps_ref = bf16[4,8,16,3456]{3,2,1,0:T(8,128)(2,1)S(1)} custom-call(bf16[64,3072]{1,0:T(8,128)(2,1)} %filters_ref.1), custom_call_target="tpu_custom_call" | custom-call | flops 25165824 | bytes 8388608 | tf_op jit(solution)/shard_map/taps/pallas_call | solution.py:127
  12.8 5.0 %all-to-all-done.x_ref = bf16[16,96,128]{2,1,0:T(8,128)(2,1)} async-done(((bf16[16,96,128]{2,1,0:T(8,128)(2,1)}), bf16[16,96,128]{2,1,0:T(8,128)(2,1)}, u32[]{:S(2)}, u32[]{:S(2)}) %all-to-all-start) | async-done | bytes 393248 | tf_op jit(solution)/shard_map/all_to_all | solution.py:355
  17.7 3.7 %conv.1 = (bf16[16,96,128]{2,1,0:T(8,128)(2,1)S(1)}, bf16[192,1024]{1,0:T(8,128)(2,1)S(1)}) custom-call(bf16[16,96,128]{2,1,0:T(8,128)(2,1)} %all-to-all-done.x_ref, bf16[4,8,16,3456]{3,2,1,0:T(8,128)(2,1)S(1)} %taps.1.taps_ref, f32[1,1024]{1,0:T(1,128)} %bitcast.1, bf16[192,1024]{1,0:T(8,128)(2,1)} %query_ref.1), custom_call_target="tpu_custom_call" | custom-call | tf_op jit(solution)/shard_map/conv/pallas_call | solution.py:201
  21.4 11.7 %all_to_all.10.packed_ref = bf16[16,96,128]{2,1,0:T(8,128)(2,1)S(1)} all-to-all(bf16[16,96,128]{2,1,0:T(8,128)(2,1)S(1)} %get-tuple-element.7), channel_id=1, replica_groups=mesh['x'=4,'ylo'=2,'core'=2,'yhi'=2,'z'=4] {'x','ylo','core'}, dimensions={0} | all-to-all | bytes 786432 | tf_op jit(solution)/shard_map/all_to_all | solution.py:359
  33.1 0.3 gate.1.refs_0_
  33.4 4.0 %collective-permute-start.3 = (bf16[192,1024]{1,0:T(8,128)(2,1)S(1)}, bf16[192,1024]{1,0:T(8,128)(2,1)S(1)}, u32[]{:S(2)}, u32[]{:S(2)}) collective-permute-start(bf16[192,1024]{1,0:T(8,128)(2,1)S(1)} %gate.1.refs_0_), channel_id=1, source_target_pairs={{0,2},{1,3},{2,0},{3,1},{4,6},{5,7},{6,4},{7,5},{8,10},{9,11},{10,... | collective-permute-start | bytes 1179656 | tf_op jit(solution)/shard_map/ppermute | solution.py:333
  37.4 2.9 %collective-permute-start = (bf16[192,1024]{1,0:T(8,128)(2,1)S(1)}, bf16[192,1024]{1,0:T(8,128)(2,1)S(1)}, u32[]{:S(2)}, u32[]{:S(2)}) collective-permute-start(bf16[192,1024]{1,0:T(8,128)(2,1)S(1)} %gate.1.refs_0_), channel_id=1, source_target_pairs={{0,4},{4,0},{1,5},{5,1},{2,6},{6,2},{3,7},{7,3},{8,12},{12,8},{9,1... | collective-permute-start | bytes 1179656 | tf_op jit(solution)/shard_map/ppermute | solution.py:336
  40.3 1.0 %collective-permute-start.5 = (bf16[192,1024]{1,0:T(8,128)(2,1)S(1)}, bf16[192,1024]{1,0:T(8,128)(2,1)S(1)}, u32[]{:S(2)}, u32[]{:S(2)}) collective-permute-start(bf16[192,1024]{1,0:T(8,128)(2,1)S(1)} %gate.1.refs_0_), channel_id=1, source_target_pairs={{0,1},{1,2},{2,3},{3,0},{4,5},{5,6},{6,7},{7,4},{8,9},{9,10},{10,1... | collective-permute-start | bytes 1179656 | tf_op jit(solution)/shard_map/ppermute | solution.py:333
  41.3 2.2 %collective-permute-start.6 = (bf16[192,1024]{1,0:T(8,128)(2,1)S(1)}, bf16[192,1024]{1,0:T(8,128)(2,1)S(1)}, u32[]{:S(2)}, u32[]{:S(2)}) collective-permute-start(bf16[192,1024]{1,0:T(8,128)(2,1)S(1)} %gate.1.refs_0_), channel_id=1, source_target_pairs={{0,3},{1,0},{2,1},{3,2},{4,7},{5,4},{6,5},{7,6},{8,11},{9,8},{10,9... | collective-permute-start | bytes 1179656 | tf_op jit(solution)/shard_map/ppermute | solution.py:333
  43.5 3.9 %collective-permute-done.3.refs_0_ = bf16[192,1024]{1,0:T(8,128)(2,1)S(1)} collective-permute-done((bf16[192,1024]{1,0:T(8,128)(2,1)S(1)}, bf16[192,1024]{1,0:T(8,128)(2,1)S(1)}, u32[]{:S(2)}, u32[]{:S(2)}) %collective-permute-start.3) | collective-permute-done | bytes 393248 | tf_op jit(solution)/shard_map/ppermute | solution.py:333
  47.4 2.9 %collective-permute-start.4 = (bf16[192,1024]{1,0:T(8,128)(2,1)S(1)}, bf16[192,1024]{1,0:T(8,128)(2,1)S(1)}, u32[]{:S(2)}, u32[]{:S(2)}) collective-permute-start(bf16[192,1024]{1,0:T(8,128)(2,1)S(1)} %collective-permute-done.3.refs_0_), channel_id=1, source_target_pairs={{0,4},{4,0},{1,5},{5,1},{2,6},{6,2},{3,7},{7,3},{8,12},{12,8},{9,1... | collective-permute-start | bytes 1179656 | tf_op jit(solution)/shard_map/ppermute | solution.py:336
  50.3 0.0 collective-permute-done.refs_1_
  50.3 1.6 %collective-permute-start.1 = (bf16[192,1024]{1,0:T(8,128)(2,1)S(1)}, bf16[192,1024]{1,0:T(8,128)(2,1)S(1)}, u32[]{:S(2)}, u32[]{:S(2)}) collective-permute-start(bf16[192,1024]{1,0:T(8,128)(2,1)S(1)} %collective-permute-done.refs_1_), channel_id=1, source_target_pairs={{0,1},{1,2},{2,3},{3,0},{4,5},{5,6},{6,7},{7,4},{8,9},{9,10},{10,1... | collective-permute-start | bytes 1179656 | tf_op jit(solution)/shard_map/ppermute | solution.py:333
  51.8 2.1 %collective-permute-start.2 = (bf16[192,1024]{1,0:T(8,128)(2,1)S(1)}, bf16[192,1024]{1,0:T(8,128)(2,1)S(1)}, u32[]{:S(2)}, u32[]{:S(2)}) collective-permute-start(bf16[192,1024]{1,0:T(8,128)(2,1)S(1)} %collective-permute-done.refs_1_), channel_id=1, source_target_pairs={{0,3},{1,0},{2,1},{3,2},{4,7},{5,4},{6,5},{7,6},{8,11},{9,8},{10,9... | collective-permute-start | bytes 1179656 | tf_op jit(solution)/shard_map/ppermute | solution.py:333
  54.0 5.9 %fetch.1.refs_1_.refs_2_ = bf16[8,1024,1024]{2,1,0:T(8,128)(2,1)S(1)} custom-call(bf16[8192,1024]{1,0:T(8,128)(2,1)} %weight_ref.1), custom_call_target="tpu_custom_call" | custom-call | bytes 16777216 | tf_op jit(solution)/shard_map/fetch/pallas_call | solution.py:319
  59.9 0.6 project.5.refs_3_
  60.5 1.0 %project.6.refs_3_ = f32[192,1024]{1,0:T(8,128)S(1)} custom-call(bf16[192,1024]{1,0:T(8,128)(2,1)S(1)} %collective-permute-done.3.refs_0_, bf16[192,1024]{1,0:T(8,128)(2,1)S(1)} %collective-permute-done.refs_1_, bf16[8,1024,1024]{2,1,0:T(8,128)(2,1)S(1)} %fetch.1.refs_1_.refs_2_, f32[192,1024]{1,0:T(8,128)S(1)} %project.5.refs_3_), custom_call_target="tpu_custom_call" | custom-call | flops 805306368 | bytes 4194304 | tf_op jit(solution)/shard_map/project/pallas_call | solution.py:280
  61.5 0.0 collective-permute-done.5.refs_0_
  61.5 0.0 collective-permute-done.6.refs_1_
  61.5 1.0 %project.7.refs_2_ = f32[192,1024]{1,0:T(8,128)S(1)} custom-call(bf16[192,1024]{1,0:T(8,128)(2,1)S(1)} %collective-permute-done.5.refs_0_, bf16[192,1024]{1,0:T(8,128)(2,1)S(1)} %collective-permute-done.6.refs_1_, bf16[8,1024,1024]{2,1,0:T(8,128)(2,1)S(1)} %fetch.1.refs_1_.refs_2_, f32[192,1024]{1,0:T(8,128)S(1)} %project.6.refs_3_), custom_call_target="tpu_custom_call" | custom-call | flops 805306368 | bytes 4194304 | tf_op jit(solution)/shard_map/project/pallas_call | solution.py:280
  62.5 0.0 collective-permute-done.4.refs_0_
  62.5 0.6 project.8.refs_3_
  63.1 0.3 collective-permute-done.1.refs_0_
  63.4 0.8 %collective-permute-done.2.refs_1_ = bf16[192,1024]{1,0:T(8,128)(2,1)S(1)} collective-permute-done((bf16[192,1024]{1,0:T(8,128)(2,1)S(1)}, bf16[192,1024]{1,0:T(8,128)(2,1)S(1)}, u32[]{:S(2)}, u32[]{:S(2)}) %collective-permute-start.2) | collective-permute-done | bytes 393248 | tf_op jit(solution)/shard_map/ppermute | solution.py:333
  64.2 1.7 %project.9 = bf16[192,1024]{1,0:T(8,128)(2,1)} custom-call(bf16[192,1024]{1,0:T(8,128)(2,1)S(1)} %collective-permute-done.1.refs_0_, bf16[192,1024]{1,0:T(8,128)(2,1)S(1)} %collective-permute-done.2.refs_1_, bf16[8,1024,1024]{2,1,0:T(8,128)(2,1)S(1)} %fetch.1.refs_1_.refs_2_, f32[192,1024]{1,0:T(8,128)S(1)} %project.8.refs_3_), custom_call_target="tpu_custom_call" | custom-call | flops 805306368 | bytes 4194304 | tf_op jit(solution)/shard_map/project/pallas_call | solution.py:280
Async XLA Ops:
  3.0 14.7 %all-to-all-start = ((bf16[16,96,128]{2,1,0:T(8,128)(2,1)}), bf16[16,96,128]{2,1,0:T(8,128)(2,1)}, u32[]{:S(2)}, u32[]{:S(2)}) async-start(bf16[16,96,128]{2,1,0:T(8,128)(2,1)} %mix.1), calls=%async_computation | async-start | bytes 786432 | tf_op jit(solution)/shard_map/all_to_all | solution.py:355
  33.4 14.0 %collective-permute-start.3 = (bf16[192,1024]{1,0:T(8,128)(2,1)S(1)}, bf16[192,1024]{1,0:T(8,128)(2,1)S(1)}, u32[]{:S(2)}, u32[]{:S(2)}) collective-permute-start(bf16[192,1024]{1,0:T(8,128)(2,1)S(1)} %gate.1.refs_0_), channel_id=1, source_target_pairs={{0,2},{1,3},{2,0},{3,1},{4,6},{5,7},{6,4},{7,5},{8,10},{9,11},{10,... | collective-permute-start | bytes 1179656 | tf_op jit(solution)/shard_map/ppermute | solution.py:333
  37.4 12.9 %collective-permute-start = (bf16[192,1024]{1,0:T(8,128)(2,1)S(1)}, bf16[192,1024]{1,0:T(8,128)(2,1)S(1)}, u32[]{:S(2)}, u32[]{:S(2)}) collective-permute-start(bf16[192,1024]{1,0:T(8,128)(2,1)S(1)} %gate.1.refs_0_), channel_id=1, source_target_pairs={{0,4},{4,0},{1,5},{5,1},{2,6},{6,2},{3,7},{7,3},{8,12},{12,8},{9,1... | collective-permute-start | bytes 1179656 | tf_op jit(solution)/shard_map/ppermute | solution.py:336
  40.3 21.2 %collective-permute-start.5 = (bf16[192,1024]{1,0:T(8,128)(2,1)S(1)}, bf16[192,1024]{1,0:T(8,128)(2,1)S(1)}, u32[]{:S(2)}, u32[]{:S(2)}) collective-permute-start(bf16[192,1024]{1,0:T(8,128)(2,1)S(1)} %gate.1.refs_0_), channel_id=1, source_target_pairs={{0,1},{1,2},{2,3},{3,0},{4,5},{5,6},{6,7},{7,4},{8,9},{9,10},{10,1... | collective-permute-start | bytes 1179656 | tf_op jit(solution)/shard_map/ppermute | solution.py:333
  41.3 20.2 %collective-permute-start.6 = (bf16[192,1024]{1,0:T(8,128)(2,1)S(1)}, bf16[192,1024]{1,0:T(8,128)(2,1)S(1)}, u32[]{:S(2)}, u32[]{:S(2)}) collective-permute-start(bf16[192,1024]{1,0:T(8,128)(2,1)S(1)} %gate.1.refs_0_), channel_id=1, source_target_pairs={{0,3},{1,0},{2,1},{3,2},{4,7},{5,4},{6,5},{7,6},{8,11},{9,8},{10,9... | collective-permute-start | bytes 1179656 | tf_op jit(solution)/shard_map/ppermute | solution.py:333
  47.4 15.1 %collective-permute-start.4 = (bf16[192,1024]{1,0:T(8,128)(2,1)S(1)}, bf16[192,1024]{1,0:T(8,128)(2,1)S(1)}, u32[]{:S(2)}, u32[]{:S(2)}) collective-permute-start(bf16[192,1024]{1,0:T(8,128)(2,1)S(1)} %collective-permute-done.3.refs_0_), channel_id=1, source_target_pairs={{0,4},{4,0},{1,5},{5,1},{2,6},{6,2},{3,7},{7,3},{8,12},{12,8},{9,1... | collective-permute-start | bytes 1179656 | tf_op jit(solution)/shard_map/ppermute | solution.py:336
  50.3 13.1 %collective-permute-start.1 = (bf16[192,1024]{1,0:T(8,128)(2,1)S(1)}, bf16[192,1024]{1,0:T(8,128)(2,1)S(1)}, u32[]{:S(2)}, u32[]{:S(2)}) collective-permute-start(bf16[192,1024]{1,0:T(8,128)(2,1)S(1)} %collective-permute-done.refs_1_), channel_id=1, source_target_pairs={{0,1},{1,2},{2,3},{3,0},{4,5},{5,6},{6,7},{7,4},{8,9},{9,10},{10,1... | collective-permute-start | bytes 1179656 | tf_op jit(solution)/shard_map/ppermute | solution.py:333
  51.8 12.3 %collective-permute-start.2 = (bf16[192,1024]{1,0:T(8,128)(2,1)S(1)}, bf16[192,1024]{1,0:T(8,128)(2,1)S(1)}, u32[]{:S(2)}, u32[]{:S(2)}) collective-permute-start(bf16[192,1024]{1,0:T(8,128)(2,1)S(1)} %collective-permute-done.refs_1_), channel_id=1, source_target_pairs={{0,3},{1,0},{2,1},{3,2},{4,7},{5,4},{6,5},{7,6},{8,11},{9,8},{10,9... | collective-permute-start | bytes 1179656 | tf_op jit(solution)/shard_map/ppermute | solution.py:333
